TPU v7x, 32 devices: a whole 2x2x4 slice. The times are simulated.
32 devices in a mesh: ctx: 8 (over z, y), fsdp: 4 (over x, core).
Axes of the slice: x: 2, y: 2, z: 4, core: 2. Of those that a mesh axis runs over, the one named last changes fastest.
Arguments:
- tokens: bfloat16 [1024, 2048], P('ctx'), may hold values from -24 to 24
- positions: int32 [1024], replicated, may hold values from 0 to 1023, each once
- pulse_indicator: int32 [2, 1024, 2048], P(None, 'ctx'), may hold values 0 or 1
- norm_gain: float32 [2048], replicated, may hold values from 0.1 to 1.9
- in_weight: bfloat16 [2048, 3, 1024], P(None, None, 'fsdp'), may hold values from -0.375 to 0.375
- out_weight: bfloat16 [1024, 2048], P('fsdp'), may hold values from -0.1875 to 0.1875
- upstream: bfloat16 [1024, 2048], P('ctx'), may hold values from -6 to 6
Outputs:
- block_out: bfloat16 [1024, 2048], P('ctx', 'fsdp')
- token_grad: float32 [1024, 2048], P('ctx', 'fsdp')
- gain_grad: float32 [2048], P('fsdp')
- in_grad: float32 [2048, 3, 1024], P('ctx', None, 'fsdp')
- out_grad: float32 [2048, 1024], P('ctx', 'fsdp')
Inputs may be any that keep to these rules, and one draw needn't show every extreme that they name: `positions`: each position of the sequence appears once.
All inputs are finite; a program needn't handle non-finite values. No bound on the sum of `pulse_indicator` on one device may be relied on, other than what follows from the above.
Results may differ from a plain program's by a relative error of at most 0.004.
The roundings to bfloat16 on the way count: a program that leaves them out, or rounds other values in their place, can miss the bound.
Values may be sent and summed in bfloat16 or wider, within the bound.
No kernel may reach another device: no remote copies, remote signals or barrier semaphores. Data moves between devices by JAX's collectives and lax.ppermute only.
A program may use at most 192 MiB of HBM per device.

v0:
```python
import jax
import jax.numpy as jnp
from jax import lax
from jax.sharding import PartitionSpec as P

HEAD_DIM = 128
TIMESTEPS = 2
SOFT_CAP = 30.0
LEAK_RATE = 0.5
THRESHOLD = 1.0
SURROGATE_SLOPE = 4.0
EPSILON = 1e-05


def leaky_forward(tokens, pulse_indicator, norm_gain):
    values = tokens.astype(jnp.float32)
    inv_rms = lax.rsqrt(jnp.mean(values * values, axis=-1, keepdims=True) + EPSILON)
    normed = values * inv_rms
    current = normed * norm_gain
    neuron_voltage = current
    voltage_trace_record = []
    pulse_number_sum = jnp.zeros_like(current)
    for present_instant in range(TIMESTEPS):
        binary_pulses = pulse_indicator[present_instant].astype(jnp.float32)
        if present_instant > 0:
            neuron_voltage = (
                LEAK_RATE
                * neuron_voltage
                * (1.0 - pulse_indicator[present_instant - 1].astype(jnp.float32))
                + current
            )
        voltage_trace_record.append(neuron_voltage)
        pulse_number_sum = pulse_number_sum + binary_pulses * neuron_voltage
    return (
        inv_rms,
        normed,
        voltage_trace_record,
        (pulse_number_sum / TIMESTEPS).astype(jnp.bfloat16),
    )


def leaky_backward(grad_rate, pulse_indicator, voltage_trace_record):
    rescaled_logits = grad_rate / TIMESTEPS
    leaky_level_prior = jnp.zeros_like(rescaled_logits)
    grad_current = jnp.zeros_like(rescaled_logits)
    for present_instant in reversed(range(TIMESTEPS)):
        binary_pulses = pulse_indicator[present_instant].astype(jnp.float32)
        capped_logits = jax.nn.sigmoid(
            SURROGATE_SLOPE * (voltage_trace_record[present_instant] - THRESHOLD)
        )
        voltage_adjoint = (
            rescaled_logits
            * (
                binary_pulses
                + voltage_trace_record[present_instant]
                * SURROGATE_SLOPE
                * capped_logits
                * (1.0 - capped_logits)
            )
            + leaky_level_prior
        )
        grad_current = grad_current + voltage_adjoint
        if present_instant > 0:
            leaky_level_prior = (
                LEAK_RATE
                * voltage_adjoint
                * (1.0 - pulse_indicator[present_instant - 1].astype(jnp.float32))
            )
    return grad_current


def body(tokens, positions, pulse_indicator, norm_gain, in_weight, out_weight, upstream):
    ctx_rank = lax.axis_index("ctx")
    fsdp_rank = lax.axis_index("fsdp")
    rows_here = tokens.shape[0]
    model_width = tokens.shape[1]
    share_cols = model_width // lax.axis_size("fsdp")
    local_width = out_weight.shape[0]
    heads_here = local_width // HEAD_DIM
    score_scale = HEAD_DIM ** (-0.5)
    own_pos = lax.dynamic_slice_in_dim(positions, ctx_rank * rows_here, rows_here)
    inv_rms, normed, voltage_trace_record, spikes = leaky_forward(
        tokens, pulse_indicator, norm_gain
    )
    flat_in = in_weight.reshape(model_width, 3 * local_width)
    project = jnp.dot(spikes, flat_in, preferred_element_type=jnp.float32).astype(jnp.bfloat16)
    project = project.reshape(rows_here, 3, local_width)
    query_flat = project[:, 0]
    queries = query_flat.reshape(rows_here, heads_here, HEAD_DIM)
    gathered = lax.all_gather(project[:, 1:], "ctx", axis=0, tiled=True)
    keys_all = gathered[:, 0].reshape(-1, heads_here, HEAD_DIM)
    values_all = gathered[:, 1].reshape(-1, heads_here, HEAD_DIM)
    allowed = positions[None, :] <= own_pos[:, None]
    scores = (
        jnp.einsum("rhd,khd->hrk", queries, keys_all, preferred_element_type=jnp.float32)
        * score_scale
    )
    squashed = jnp.tanh(scores / SOFT_CAP)
    exponent = jnp.where(allowed[None], jnp.exp(SOFT_CAP * squashed), 0.0)
    totals = jnp.sum(exponent, axis=-1, keepdims=True)
    attn_prob = exponent / totals
    prob_low = attn_prob.astype(jnp.bfloat16)
    attended = jnp.einsum("hrk,khd->rhd", prob_low, values_all, preferred_element_type=jnp.float32)
    attended = attended.astype(jnp.bfloat16).reshape(rows_here, local_width)
    partial_out = jnp.dot(attended, out_weight, preferred_element_type=jnp.float32)
    summed_out = lax.psum_scatter(partial_out, "fsdp", scatter_dimension=1, tiled=True)
    low_col = fsdp_rank * share_cols
    token_share = lax.dynamic_slice_in_dim(tokens, low_col, share_cols, 1).astype(jnp.float32)
    block_out = (token_share + summed_out).astype(jnp.bfloat16)
    grad_attn = jnp.dot(upstream, out_weight.T, preferred_element_type=jnp.float32).astype(
        jnp.bfloat16
    )
    grad_heads = grad_attn.reshape(rows_here, heads_here, HEAD_DIM)
    grad_prob = jnp.einsum(
        "rhd,khd->hrk", grad_heads, values_all, preferred_element_type=jnp.float32
    )
    delta = jnp.sum(attn_prob * grad_prob, axis=-1, keepdims=True)
    score_grad = (
        attn_prob * (grad_prob - delta) * (1.0 - squashed * squashed) * score_scale
    ).astype(jnp.bfloat16)
    grad_query = jnp.einsum(
        "hrk,khd->rhd", score_grad, keys_all, preferred_element_type=jnp.float32
    )
    grad_query = grad_query.astype(jnp.bfloat16).reshape(rows_here, local_width)
    grad_keys = jnp.einsum("hrk,rhd->khd", score_grad, queries, preferred_element_type=jnp.float32)
    grad_values = jnp.einsum(
        "hrk,rhd->khd", prob_low, grad_heads, preferred_element_type=jnp.float32
    )
    key_grads = lax.psum_scatter(
        jnp.stack(
            [
                grad_keys.reshape(rows_here * lax.axis_size("ctx"), local_width),
                grad_values.reshape(rows_here * lax.axis_size("ctx"), local_width),
            ],
            axis=1,
        ),
        "ctx",
        scatter_dimension=0,
        tiled=True,
    )
    grad_project = jnp.concatenate([grad_query[:, None], key_grads.astype(jnp.bfloat16)], axis=1)
    flat_grad = grad_project.reshape(rows_here, 3 * local_width)
    spike_part = jnp.dot(flat_grad, flat_in.T, preferred_element_type=jnp.float32)
    grad_spikes = lax.psum(spike_part, "fsdp")
    grad_current = leaky_backward(grad_spikes, pulse_indicator, voltage_trace_record)
    scaled_grad = grad_current * norm_gain
    row_mean = jnp.mean(scaled_grad * normed, axis=-1, keepdims=True)
    full_grad = upstream.astype(jnp.float32) + inv_rms * (scaled_grad - normed * row_mean)
    token_grad = lax.dynamic_slice_in_dim(full_grad, low_col, share_cols, 1)
    gain_part = lax.dynamic_slice_in_dim(
        jnp.sum(grad_current * normed, axis=0), low_col, share_cols
    )
    gain_grad = lax.psum(gain_part, "ctx")
    grad_inward = jnp.einsum("rc,rk->ck", spikes, flat_grad, preferred_element_type=jnp.float32)
    grad_outward = jnp.einsum("rc,rk->ck", upstream, attended, preferred_element_type=jnp.float32)
    weight_rows = lax.psum_scatter(
        jnp.concatenate([grad_inward, grad_outward], axis=1), "ctx", scatter_dimension=0, tiled=True
    )
    in_grad = weight_rows[:, : 3 * local_width].reshape(-1, 3, local_width)
    out_grad = weight_rows[:, 3 * local_width :]
    return (block_out, token_grad, gain_grad, in_grad, out_grad)


def solution(mesh):
    placed = (
        P("ctx", None),
        P(),
        P(None, "ctx", None),
        P(),
        P(None, None, "fsdp"),
        P("fsdp", None),
        P("ctx", None),
    )
    return jax.shard_map(
        body,
        mesh=mesh,
        in_specs=placed,
        out_specs=(
            P("ctx", "fsdp"),
            P("ctx", "fsdp"),
            P("fsdp"),
            P("ctx", None, "fsdp"),
            P("ctx", "fsdp"),
        ),
        check_vma=False,
    )
```

profile of v0, /device:TPU:0, one launch (start us, length us, event | category | flops | bytes accessed | tf_op | source)
XLA Modules:
  0.0 375.2 jit_solution(12632375523382011827)
XLA Ops:
  7.2 1.3 fusion.7
  8.6 4.9 %copy.23 = bf16[2048,3,256]{0,2,1:T(8,128)(2,1)} copy(bf16[2048,3,256]{2,0,1:T(8,128)(2,1)} %param.11) | data formatting | bytes 6291456 | tf_op args[4]
  13.4 2.7 convert_multiply_fusion
  16.9 1.2 convolution_convert_fusion
  19.1 1.5 convolution_convert_fusion.2
  21.0 40.4 %all-gather.2.cloned.1.call-done = bf16[1024,2,256]{0,2,1:T(8,128)(2,1)} async-done(((bf16[128,2,256]{0,2,1:T(8,128)(2,1)}), bf16[1024,2,256]{0,2,1:T(8,128)(2,1)}) %all-gather.2.cloned.1.call-update) | async-done | bytes 1048592 | tf_op jit(solution)/shard_map/all_gather | solution.py:90
  61.4 1.3 fusion.44
  63.4 1.3 fusion.46
  65.4 1.0 copy-done.8
  66.4 1.5 fusion.29
  67.9 4.2 %fusion.17 = f32[2,128,1024]{2,1,0:T(8,128)} fusion(bf16[128,2,128]{0,2,1:T(8,128)(2,1)S(1)} %bitcast.88, f32[2,128,1024]{2,1,0:T(8,128)} %fusion.46, f32[2,128,1024]{2,1,0:T(8,128)} %copy-done.8, f32[2,128]{1,0:T(2,128)S(1)} %get-tuple-element.22, pred[128,1024]{1,0:T(8,128)(4,1)S(1)} %broadcast_compare_fusion), kind=kOutput, calls=%fused_computation.37 | convolution fusion | flops 70780160 | bytes 3343360 | tf_op jit(solution)/shard_map/hrk,rhd->khd/dot_general | solution.py:125
  72.2 2.5 copy.31
  74.7 2.6 copy.30
  77.3 3.0 pad_maximum_fusion.1
  80.4 1.8 convolution_convert_fusion.3
  82.2 1.3 fusion.45
  83.6 3.4 convolution_convert_fusion.1
  87.1 2.9 convolution_bitcast_fusion
  89.9 57.2 %reduce-scatter.6.cloned.1.call-done = f32[128,2,256]{2,0,1:T(8,128)} async-done(((f32[1024,2,256]{2,0,1:T(8,128)}), f32[128,2,256]{2,0,1:T(8,128)}) %reduce-scatter.6.cloned.1.call-update) | async-done | bytes 262160 | tf_op jit(solution)/shard_map/reduce_scatter | solution.py:129
  148.8 1.1 copy.33
  149.9 4.0 %convolution_bitcast_fusion.1 = f32[128,2048]{1,0:T(8,128)} fusion(bf16[2048,3,256]{2,0,1:T(8,128)(2,1)} %param.11, bf16[128,2,256]{2,0,1:T(8,128)(2,1)S(1)} %convert_element_type.75, bf16[128,1,256]{2,0,1:T(8,128)(2,1)S(1)} %copy.32), kind=kOutput, calls=%fused_computation.3 | convolution fusion | flops 402751488 | bytes 4390912 | tf_op jit(solution)/shard_map/dot_general | solution.py:143
  154.0 2.0 fusion.47
  156.0 6.2 %pad_maximum_fusion = f32[2048,1024]{0,1:T(8,128)} fusion(f32[2048,256]{0,1:T(8,128)} %convolution_bitcast_fusion, f32[2048,768]{0,1:T(8,128)S(1)} %fusion.47), kind=kLoop, calls=%fused_computation.1 | loop fusion | flops 2097152 | bytes 16777216 | tf_op jit(solution)/shard_map/concatenate | solution.py:157
  162.2 11.4 %reduce-scatter.4.cloned.1.call-done = f32[128,512]{1,0:T(8,128)} async-done(((f32[128,2048]{1,0:T(8,128)}), f32[128,512]{1,0:T(8,128)}) %reduce-scatter.4.cloned.1.call-update) | async-done | bytes 262160 | tf_op jit(solution)/shard_map/reduce_scatter | solution.py:106
  173.6 1.7 add_convert_fusion
  175.3 36.8 %all-reduce.2.cloned.1.call-done = f32[128,2048]{1,0:T(8,128)} async-done(((f32[128,2048]{1,0:T(8,128)}), f32[128,2048]{1,0:T(8,128)}) %all-reduce.2.cloned.1.call-update) | async-done | bytes 1048592 | tf_op jit(solution)/shard_map/psum | solution.py:144
  212.1 3.9 %multiply_reduce_fusion = (f32[2048]{0:T(1024)S(1)}, f32[128]{0:T(128)S(1)}, f32[128,2048]{1,0:T(8,128)}) fusion(bf16[128,2048]{1,0:T(8,128)(2,1)} %param.7, f32[128]{0:T(128)S(1)} %add_rsqrt_fusion, f32[2048]{0:T(1024)S(1)} %copy-done.6, s32[2,128,2048]{2,1,0:T(8,128)S(1)} %copy-done.2, f32[128,2048]{1,0:T(8,128)} %all-reduce.2.cloned.1.call-done), kind=kLoop, calls=%fused_computation.31 | loop fusion | flops 10745728 | bytes 4736000 | tf_op jit(solution)/shard_map/reduce_sum | solution.py:151
  216.1 22.3 %psum.15 = f32[512]{0:T(512)} all-reduce(f32[512]{0:T(512)S(1)} %dynamic_slice.15), channel_id=1, replica_groups=mesh['ctx'=8,'fsdp'=4] {'ctx'}, use_global_device_ids=true, to_apply=%region_8.9 | all-reduce | flops 512 | bytes 4096 | tf_op jit(solution)/shard_map/psum | solution.py:153
  238.4 1.9 fusion.28
  240.3 125.2 %reduce-scatter.8.cloned.1.call-done = f32[256,1024]{0,1:T(8,128)} async-done(((f32[2048,1024]{0,1:T(8,128)}), f32[256,1024]{0,1:T(8,128)}) %reduce-scatter.8.cloned.1.call-update) | async-done | bytes 1048592 | tf_op jit(solution)/shard_map/reduce_scatter | solution.py:156
  365.5 1.2 slice.40
  366.7 1.1 copy.34
  (43 shorter events, 6.4 us)
Async XLA Ops:
  7.2 11.9 %copy-start = (bf16[256,2048]{1,0:T(8,128)(2,1)S(1)}, bf16[256,2048]{1,0:T(8,128)(2,1)}, u32[]{:S(2)}) copy-start(bf16[256,2048]{1,0:T(8,128)(2,1)} %param.12) | copy-start | bytes 3145732
  7.2 54.2 %all-gather.2.cloned.1.call-start = ((), (), s32[]{:S(2)}) async-start(), calls=%async_computation.3 | async-start | bytes 1179648 | tf_op jit(solution)/shard_map/all_gather | solution.py:90
  8.5 4.9 %copy-start.2 = (s32[2,128,2048]{2,1,0:T(8,128)S(1)}, s32[2,128,2048]{2,1,0:T(8,128)}, u32[]{:S(2)}) copy-start(s32[2,128,2048]{2,1,0:T(8,128)} %param.9) | copy-start | bytes 6291460
  8.6 4.9 %copy-start.6 = (f32[2048]{0:T(1024)S(1)}, f32[2048]{0:T(1024)}, u32[]{:S(2)}) copy-start(f32[2048]{0:T(1024)} %param.10) | copy-start | bytes 24580
  13.4 3.5 copy-start.1
  16.1 0.8 copy-start.3
  16.9 3.8 %copy-start.7 = (s32[1024]{0:T(1024)S(1)}, s32[1024]{0:T(1024)}, u32[]{:S(2)}) copy-start(s32[1024]{0:T(1024)} %param.8) | copy-start | bytes 12292
  19.0 128.2 %reduce-scatter.6.cloned.1.call-start = ((), (), s32[]{:S(2)}) async-start(), calls=%async_computation.5 | async-start | bytes 2359296 | tf_op jit(solution)/shard_map/reduce_scatter | solution.py:129
  62.6 0.8 copy-start.4
  62.7 2.1 copy-start.5
  65.4 1.0 copy-start.8
  80.3 93.3 %reduce-scatter.4.cloned.1.call-start = ((), (), s32[]{:S(2)}) async-start(), calls=%async_computation.4 | async-start | bytes 1310720 | tf_op jit(solution)/shard_map/reduce_scatter | solution.py:106
  83.6 128.5 %all-reduce.2.cloned.1.call-start = ((), (), s32[]{:S(2)}) async-start(), calls=%async_computation.6 | async-start | bytes 2097152 | tf_op jit(solution)/shard_map/psum | solution.py:144
  153.9 211.6 %reduce-scatter.8.cloned.1.call-start = ((), (), s32[]{:S(2)}) async-start(), calls=%async_computation.7 | async-start | bytes 9437184 | tf_op jit(solution)/shard_map/reduce_scatter | solution.py:156
  365.5 2.4 slice-start
Sparse Core Ops, SparseCore 0:
  19.1 42.2 all-gather.1
  80.4 66.6 reduce-scatter.5
  149.7 23.8 reduce-scatter.3
  176.0 36.0 all-reduce.1
  215.6 149.8 reduce-scatter.7
where the time goes:
time: 376 us; the launch traced here: 375 us
  waiting for transfers between devices  271 us (72%)
  matrix products  25.8 us (7%)
  other arithmetic  22.5 us (6%)
  blocking collectives  22.3 us (6%)
  local copies, waits for them, and re-layouts  19.3 us (5%)
  between operations  14 us (4%)
    reduce_scatter x1, waiting for transfers between devices, body(): lax.psum_scatter(jnp.concatenate([grad_inward, grad_outward], axis=1), 'c...  125 us
    reduce_scatter x1, waiting for transfers between devices, body(): lax.psum_scatter(jnp.stack([grad_keys.reshape(rows_here * lax.axis_size('...  57.2 us
    all_gather x1, waiting for transfers between devices, body(): gathered = lax.all_gather(project[:, 1:], 'ctx', axis=0, tiled=True)  40.4 us
    psum x1, waiting for transfers between devices, body(): grad_spikes = lax.psum(spike_part, 'fsdp')  36.8 us
    psum x1, blocking collectives, body(): gain_grad = lax.psum(gain_part, 'ctx')  22.3 us
    reduce_scatter x1, waiting for transfers between devices, body(): lax.psum_scatter(partial_out, 'fsdp', scatter_dimension=1, tiled=True)  11.4 us
    unnamed x21, local copies, waits for them, and re-layouts  9.44 us
  transfers between devices with their start and end apart: 5, of which 5 were waited for; matrix products, arithmetic and copies ran while one was open for 9% of the time, Pallas kernels for 0%

commit v1 on v0

--- a/solution.py
+++ b/solution.py
@@ -10,6 +10,20 @@
 THRESHOLD = 1.0
 SURROGATE_SLOPE = 4.0
 EPSILON = 1e-05
+
+
+def step_on_the_skins(incoming_x, shard_axis, row_dim):
+    n_chips = jax.lax.axis_size(shard_axis)
+    return jax.lax.all_to_all(
+        jnp.tile(
+            incoming_x,
+            tuple((n_chips if to_i == row_dim else 1 for to_i in range(incoming_x.ndim))),
+        ),
+        concat_axis=row_dim,
+        axis_name=shard_axis,
+        split_axis=row_dim,
+        tiled=True,
+    )
 
 
 def leaky_forward(tokens, pulse_indicator, norm_gain):
@@ -87,7 +101,7 @@
     project = project.reshape(rows_here, 3, local_width)
     query_flat = project[:, 0]
     queries = query_flat.reshape(rows_here, heads_here, HEAD_DIM)
-    gathered = lax.all_gather(project[:, 1:], "ctx", axis=0, tiled=True)
+    gathered = step_on_the_skins(project[:, 1:], "ctx", 0)
     keys_all = gathered[:, 0].reshape(-1, heads_here, HEAD_DIM)
     values_all = gathered[:, 1].reshape(-1, heads_here, HEAD_DIM)
     allowed = positions[None, :] <= own_pos[:, None]

time: 376 us -> 369 us (0.981)
  waiting for transfers between devices: 271 us -> 259 us
  starting transfers between devices: 0.21 us -> 7.62 us
  local copies, waits for them, and re-layouts: 19.3 us -> 23.5 us
    all_gather x1 -> x0, waiting for transfers between devices: 40.4 us -> none  [body(): gathered = lax.all_gather(project[:, 1:], 'ctx', axis=0, tiled=True)]
    all_to_all x0 -> x1, waiting for transfers between devices: none -> 24.8 us  [step_on_the_skins(): jax.lax.all_to_all(jnp.tile(incoming_x, tuple((n_chips if to_i == row_dim...]
    all_to_all x0 -> x1, starting transfers between devices: none -> 7.28 us  [step_on_the_skins(): jax.lax.all_to_all(jnp.tile(incoming_x, tuple((n_chips if to_i == row_dim...]
    unnamed x21 -> x28, local copies, waits for them, and re-layouts: 9.44 us -> 12.2 us
  transfers between devices with their start and end apart: 5 -> 5, of which waited for: 5 -> 5; matrix products, arithmetic and copies ran while one was open for 9% -> 8% of each run, Pallas kernels for 0% -> 0%
where the time goes in v1:
time: 369 us
  waiting for transfers between devices  259 us (70%)
  local copies, waits for them, and re-layouts  23.5 us (6%)
  matrix products  23.1 us (6%)
  blocking collectives  22.4 us (6%)
  other arithmetic  19.2 us (5%)
  between operations  14 us (4%)
  starting transfers between devices  7.62 us (2%)
    reduce_scatter x1, waiting for transfers between devices, body(): lax.psum_scatter(jnp.concatenate([grad_inward, grad_outward], axis=1), 'c...  125 us
    reduce_scatter x1, waiting for transfers between devices, body(): lax.psum_scatter(jnp.stack([grad_keys.reshape(rows_here * lax.axis_size('...  58.8 us
    psum x1, waiting for transfers between devices, body(): grad_spikes = lax.psum(spike_part, 'fsdp')  36.9 us
    all_to_all x1, waiting for transfers between devices, step_on_the_skins(): jax.lax.all_to_all(jnp.tile(incoming_x, tuple((n_chips if to_i == row_dim...  24.8 us
    psum x1, blocking collectives, body(): gain_grad = lax.psum(gain_part, 'ctx')  22.4 us
    reduce_scatter x1, waiting for transfers between devices, body(): lax.psum_scatter(partial_out, 'fsdp', scatter_dimension=1, tiled=True)  13.1 us
    unnamed x28, local copies, waits for them, and re-layouts  12.2 us
  transfers between devices with their start and end apart: 5, of which 5 were waited for; matrix products, arithmetic and copies ran while one was open for 8% of the time, Pallas kernels for 0%

profile of v1, /device:TPU:0, one launch (start us, length us, event | category | flops | bytes accessed | tf_op | source)
XLA Modules:
  0.0 368.6 jit_solution(6875663364809647980)
XLA Ops:
  7.2 1.3 fusion.7
  8.5 4.9 %copy.36 = bf16[2048,3,256]{0,2,1:T(8,128)(2,1)} copy(bf16[2048,3,256]{2,0,1:T(8,128)(2,1)} %param.11) | data formatting | bytes 6291456 | tf_op args[4]
  13.4 2.8 convert_multiply_fusion
  17.0 1.2 convolution_convert_fusion
  18.5 1.5 tile.4
  20.1 7.3 %all-to-all-start = ((bf16[1024,2,256]{2,1,0:T(2,128)(2,1)}), bf16[1024,2,256]{2,1,0:T(2,128)(2,1)S(1)}, u32[]{:S(2)}, u32[]{:S(2)}) async-start(bf16[1024,2,256]{2,1,0:T(2,128)(2,1)} %bitcast.4), calls=%async_computation | async-start | bytes 2097152 | tf_op jit(solution)/shard_map/all_to_all | solution.py:17
  28.3 24.8 %all-to-all-done = bf16[1024,2,256]{2,1,0:T(2,128)(2,1)S(1)} async-done(((bf16[1024,2,256]{2,1,0:T(2,128)(2,1)}), bf16[1024,2,256]{2,1,0:T(2,128)(2,1)S(1)}, u32[]{:S(2)}, u32[]{:S(2)}) %all-to-all-start) | async-done | bytes 1048608 | tf_op jit(solution)/shard_map/all_to_all | solution.py:17
  53.1 2.3 fusion.44
  55.4 3.5 copy.55
  58.9 1.3 copy.39
  60.6 2.0 fusion.22
  63.6 1.5 fusion.29
  65.1 3.7 fusion.17
  68.8 1.6 copy.47
  70.4 1.6 copy.46
  71.9 1.5 pad_maximum_fusion.1
  73.5 1.9 convolution_convert_fusion.3
  75.4 1.3 fusion.45
  76.8 3.2 convolution_convert_fusion.1
  80.1 1.5 convolution_bitcast_fusion
  81.6 58.8 %reduce-scatter.6.cloned.1.call-done = f32[128,2,256]{2,0,1:T(8,128)} async-done(((f32[1024,2,256]{2,0,1:T(8,128)}), f32[128,2,256]{2,0,1:T(8,128)}) %reduce-scatter.6.cloned.1.call-update) | async-done | bytes 262160 | tf_op jit(solution)/shard_map/reduce_scatter | solution.py:143
  143.1 4.1 %convolution_bitcast_fusion.1 = f32[128,2048]{1,0:T(8,128)} fusion(bf16[2048,3,256]{2,0,1:T(8,128)(2,1)} %param.11, bf16[128,2,256]{2,0,1:T(8,128)(2,1)S(1)} %convert_element_type.75, bf16[128,1,256]{2,0,1:T(8,128)(2,1)S(1)} %copy.48), kind=kOutput, calls=%fused_computation.3 | convolution fusion | flops 402751488 | bytes 4390912 | tf_op jit(solution)/shard_map/dot_general | solution.py:157
  147.4 2.0 fusion.47
  149.4 4.3 %pad_maximum_fusion = f32[2048,1024]{0,1:T(8,128)} fusion(f32[2048,256]{0,1:T(8,128)S(1)} %convolution_bitcast_fusion, f32[2048,768]{0,1:T(8,128)S(1)} %fusion.47), kind=kLoop, calls=%fused_computation.1 | loop fusion | flops 2097152 | bytes 16777216 | tf_op jit(solution)/shard_map/concatenate | solution.py:171
  153.7 13.1 %reduce-scatter.4.cloned.1.call-done = f32[128,512]{1,0:T(8,128)} async-done(((f32[128,2048]{1,0:T(8,128)}), f32[128,512]{1,0:T(8,128)}) %reduce-scatter.4.cloned.1.call-update) | async-done | bytes 262160 | tf_op jit(solution)/shard_map/reduce_scatter | solution.py:120
  166.8 1.7 add_convert_fusion
  168.5 36.9 %all-reduce.2.cloned.1.call-done = f32[128,2048]{1,0:T(8,128)} async-done(((f32[128,2048]{1,0:T(8,128)}), f32[128,2048]{1,0:T(8,128)}) %all-reduce.2.cloned.1.call-update) | async-done | bytes 1048592 | tf_op jit(solution)/shard_map/psum | solution.py:158
  205.4 3.9 %multiply_reduce_fusion = (f32[2048]{0:T(1024)S(1)}, f32[128]{0:T(128)S(1)}, f32[128,2048]{1,0:T(8,128)}) fusion(bf16[128,2048]{1,0:T(8,128)(2,1)} %param.7, f32[128]{0:T(128)S(1)} %add_rsqrt_fusion, f32[2048]{0:T(1024)S(1)} %copy-done.9, s32[2,128,2048]{2,1,0:T(8,128)S(1)} %copy-done.3, f32[128,2048]{1,0:T(8,128)} %all-reduce.2.cloned.1.call-done), kind=kLoop, calls=%fused_computation.31 | loop fusion | flops 10745728 | bytes 4736000 | tf_op jit(solution)/shard_map/reduce_sum | solution.py:165
  209.4 22.4 %psum.15 = f32[512]{0:T(512)} all-reduce(f32[512]{0:T(512)S(1)} %dynamic_slice.15), channel_id=1, replica_groups=mesh['ctx'=8,'fsdp'=4] {'ctx'}, use_global_device_ids=true, to_apply=%region_8.9 | all-reduce | flops 512 | bytes 4096 | tf_op jit(solution)/shard_map/psum | solution.py:167
  231.9 1.9 fusion.28
  233.8 125.0 %reduce-scatter.8.cloned.1.call-done = f32[256,1024]{0,1:T(8,128)} async-done(((f32[2048,1024]{0,1:T(8,128)}), f32[256,1024]{0,1:T(8,128)}) %reduce-scatter.8.cloned.1.call-update) | async-done | bytes 1048592 | tf_op jit(solution)/shard_map/reduce_scatter | solution.py:170
  358.8 1.2 slice.40
  (52 shorter events, 8.7 us)
Async XLA Ops:
  7.2 20.3 %copy-start = (bf16[256,2048]{1,0:T(8,128)(2,1)S(1)}, bf16[256,2048]{1,0:T(8,128)(2,1)}, u32[]{:S(2)}) copy-start(bf16[256,2048]{1,0:T(8,128)(2,1)} %param.12) | copy-start | bytes 3145732
  8.5 4.9 %copy-start.2 = (s32[2,128,2048]{2,1,0:T(8,128)S(1)}, s32[2,128,2048]{2,1,0:T(8,128)}, u32[]{:S(2)}) copy-start(s32[2,128,2048]{2,1,0:T(8,128)} %param.9) | copy-start | bytes 6291460
  8.5 4.9 %copy-start.9 = (f32[2048]{0:T(1024)S(1)}, f32[2048]{0:T(1024)}, u32[]{:S(2)}) copy-start(f32[2048]{0:T(1024)} %param.10) | copy-start | bytes 24580
  13.4 3.6 copy-start.1
  16.2 0.8 copy-start.4
  17.0 10.4 %copy-start.5 = (bf16[128,2048]{1,0:T(8,128)(2,1)S(1)}, bf16[128,2048]{1,0:T(8,128)(2,1)}, u32[]{:S(2)}) copy-start(bf16[128,2048]{1,0:T(8,128)(2,1)} %param.13) | copy-start | bytes 1572868
  18.2 9.9 %copy-start.10 = (s32[1024]{0:T(1024)S(1)}, s32[1024]{0:T(1024)}, u32[]{:S(2)}) copy-start(s32[1024]{0:T(1024)} %param.8) | copy-start | bytes 12292
  20.1 33.0 %all-to-all-start = ((bf16[1024,2,256]{2,1,0:T(2,128)(2,1)}), bf16[1024,2,256]{2,1,0:T(2,128)(2,1)S(1)}, u32[]{:S(2)}, u32[]{:S(2)}) async-start(bf16[1024,2,256]{2,1,0:T(2,128)(2,1)} %bitcast.4), calls=%async_computation | async-start | bytes 2097152 | tf_op jit(solution)/shard_map/all_to_all | solution.py:17
  27.4 113.0 %reduce-scatter.6.cloned.1.call-start = ((), (), s32[]{:S(2)}) async-start(), calls=%async_computation.5 | async-start | bytes 2359296 | tf_op jit(solution)/shard_map/reduce_scatter | solution.py:143
  60.2 4.9 %copy-start.6 = (bf16[1024,1,256]{0,2,1:T(8,128)(2,1)}, bf16[1024,1,256]{0,2,1:T(8,128)(2,1)S(1)}, u32[]{:S(2)}) copy-start(bf16[1024,1,256]{0,2,1:T(8,128)(2,1)S(1)} %copy.39) | copy-start | bytes 1572868
  60.6 4.6 %copy-start.7 = (f32[2,128,1024]{2,1,0:T(8,128)}, f32[2,128,1024]{2,1,0:T(8,128)S(1)}, u32[]{:S(2)}) copy-start(f32[2,128,1024]{2,1,0:T(8,128)S(1)} %fusion.46) | copy-start | bytes 3145732
  62.7 1.0 copy-start.11
  73.4 3.3 copy-start.8
  73.5 93.4 %reduce-scatter.4.cloned.1.call-start = ((), (), s32[]{:S(2)}) async-start(), calls=%async_computation.4 | async-start | bytes 1310720 | tf_op jit(solution)/shard_map/reduce_scatter | solution.py:120
  76.7 128.7 %all-reduce.2.cloned.1.call-start = ((), (), s32[]{:S(2)}) async-start(), calls=%async_computation.6 | async-start | bytes 2097152 | tf_op jit(solution)/shard_map/psum | solution.py:158
  147.2 211.6 %reduce-scatter.8.cloned.1.call-start = ((), (), s32[]{:S(2)}) async-start(), calls=%async_computation.7 | async-start | bytes 9437184 | tf_op jit(solution)/shard_map/reduce_scatter | solution.py:170
  153.7 51.7 %copy-start.3 = (s32[2,128,2048]{2,1,0:T(8,128)S(1)}, s32[2,128,2048]{2,1,0:T(8,128)}, u32[]{:S(2)}) copy-start(s32[2,128,2048]{2,1,0:T(8,128)} %param.9) | copy-start | bytes 6291460
  358.8 2.4 slice-start
Sparse Core Ops, SparseCore 0:
  73.6 66.7 reduce-scatter.5
  142.9 23.9 reduce-scatter.3
  169.3 36.0 all-reduce.1
  208.9 149.8 reduce-scatter.7
